TPU v7x, 128 devices: a whole 4x4x4 slice. The times are simulated.
128 devices in a mesh: mic: 8 (over x_lo, z), tm: 16 (over x_hi, y, core).
Axes of the slice: x: 4 (x_hi: 2, x_lo: 2; x = x_hi * 2 + x_lo), y: 4, z: 4, core: 2. Of those that a mesh axis runs over, the one named last changes fastest.
Arguments:
- signal: float32 [8, 16384, 512], P('mic', 'tm'), may hold values from -6 to 6
- conv_weight: float32 [2, 3, 2, 512, 512], replicated, may hold values from -0.1875 to 0.1875
- conv_bias: float32 [2, 3, 512], replicated, may hold values from -3 to 3
- transform_in: float32 [2, 512, 512], replicated, may hold values from -0.25 to 0.25
- transform_mid: float32 [2, 512, 512], replicated, may hold values from -0.25 to 0.25
- transform_out: float32 [2, 1024, 512], replicated, may hold values from -0.1875 to 0.1875
- transform_offsets_bias: float32 [2, 3, 512], replicated, may hold values from -3 to 3
Outputs:
- separated: float32 [8, 16384, 512], P('mic', 'tm')
All inputs are finite; a program needn't handle non-finite values.
Results may differ from a plain program's by a relative error of at most 0.0001.
Values sent between devices are 32-bit elements; how exact they have to be, the bound alone decides.
No kernel may reach another device: no remote copies, remote signals or barrier semaphores. Data moves between devices by JAX's collectives and lax.ppermute only.
A program may use at most 128 MiB of HBM per device.

v0:
```python
import jax
import jax.numpy as jnp
from jax import lax
from jax.sharding import PartitionSpec as P

SEPARATOR_BLOCKS = 2


def from_behind(x, axis, by):
    length = lax.axis_size(axis)
    pairs = [(i, i + by) for i in range(length) if 0 <= i + by < length]
    return lax.ppermute(x, axis, pairs)


def matmul(left, right):
    return jnp.dot(left, right, precision=lax.Precision.HIGHEST, preferred_element_type=jnp.float32)


def convolve(hidden_activations, weights, bias, delayed):
    return hidden_activations + jnp.tanh(
        matmul(hidden_activations, weights[0]) + matmul(delayed, weights[1]) + bias
    )


def body(
    signal,
    conv_weight,
    conv_bias,
    transform_in,
    transform_mid,
    transform_out,
    transform_offsets_bias,
):
    hidden_activations = signal[0]
    frames = hidden_activations.shape[0]
    half = frames // 2
    channels = hidden_activations.shape[1]
    micro_count = jnp.float32(lax.axis_size("mic") * signal.shape[0])
    for section_index in range(SEPARATOR_BLOCKS):
        earlier = from_behind(hidden_activations, "tm", 1)[frames - half :]
        delayed = jnp.concatenate([earlier, hidden_activations[: frames - half]], axis=0)
        hidden_activations = convolve(
            hidden_activations, conv_weight[section_index, 0], conv_bias[section_index, 0], delayed
        )
        delayed = from_behind(hidden_activations, "tm", 1)
        hidden_activations = convolve(
            hidden_activations, conv_weight[section_index, 1], conv_bias[section_index, 1], delayed
        )
        delayed = from_behind(hidden_activations, "tm", 2)
        hidden_activations = convolve(
            hidden_activations, conv_weight[section_index, 2], conv_bias[section_index, 2], delayed
        )
        mapped = jnp.tanh(
            matmul(hidden_activations, transform_in[section_index])
            + transform_offsets_bias[section_index, 0]
        )
        summed = lax.psum(mapped, "mic")
        pooled = jnp.tanh(
            matmul(summed / micro_count, transform_mid[section_index])
            + transform_offsets_bias[section_index, 1]
        )
        mixing = (
            matmul(mapped, transform_out[section_index, :channels])
            + matmul(pooled, transform_out[section_index, channels:])
            + transform_offsets_bias[section_index, 2]
        )
        hidden_activations = hidden_activations + jnp.tanh(mixing)
    return hidden_activations[None]


def solution(mesh):
    placed = (P("mic", "tm", None), P(), P(), P(), P(), P(), P())
    return jax.shard_map(
        body, mesh=mesh, in_specs=placed, out_specs=P("mic", "tm", None), check_vma=False
    )
```

profile of v0, /device:TPU:0, one launch (start us, length us, event | category | flops | bytes accessed | tf_op | source)
XLA Modules:
  0.0 462.4 jit_solution(18367661636955650479)
XLA Ops:
  6.5 1.5 collective-permute-start
  8.1 0.8 fusion.78
  8.9 1.3 slice_bitcast_fusion
  10.2 4.7 %fusion.46 = f32[1024,512]{1,0:T(8,128)S(1)} fusion(f32[2,3,2,512,512]{4,3,2,1,0:T(8,128)} %param.8, f32[1,1024,512]{2,1,0:T(8,128)S(1)} %copy-done.2), kind=kOutput, calls=%fused_computation.52 | convolution fusion | flops 3221225472 | bytes 5242880 | tf_op jit(solution)/shard_map/dot_general | solution.py:16
  15.0 4.9 %tanh_add_fusion.6 = f32[1024,512]{1,0:T(8,128)S(1)} fusion(f32[1024,512]{1,0:T(8,128)S(1)} %fusion.46, f32[512,512]{1,0:T(8,128)S(1)} %slice_bitcast_fusion, f32[512,512]{1,0:T(8,128)S(1)} %slice.178, f32[512]{0:T(512)S(1)} %bitcast.105, f32[2,3,2,512,512]{4,3,2,1,0:T(8,128)} %param.8, f32[1,1024,512]{2,1,0:T(8,128)S(1)} %copy-done.2), kind=kOutput, calls=%fused_computation.27 | convolution fusion | flops 3223322624 | bytes 9439232 | tf_op jit(solution)/shard_map/dot_general | solution.py:16
  19.9 21.0 %collective-permute-start.1 = (f32[1024,512]{1,0:T(8,128)S(1)}, f32[1024,512]{1,0:T(8,128)S(1)}, u32[]{:S(2)}, u32[]{:S(2)}) collective-permute-start(f32[1024,512]{1,0:T(8,128)S(1)} %tanh_add_fusion.6), channel_id=1, source_target_pairs={{0,1},{1,2},{2,3},{3,4},{4,5},{5,6},{6,7},{7,8},{8,9},{9,10},{10,1... | collective-permute-start | bytes 6291464 | tf_op jit(solution)/shard_map/ppermute | solution.py:12
  40.9 4.7 %fusion.43 = f32[1024,512]{1,0:T(8,128)S(1)} fusion(f32[1024,512]{1,0:T(8,128)S(1)} %tanh_add_fusion.6, f32[2,3,2,512,512]{4,3,2,1,0:T(8,128)} %param.8), kind=kOutput, calls=%fused_computation.49 | convolution fusion | flops 3221225472 | bytes 5242880 | tf_op jit(solution)/shard_map/dot_general | solution.py:16
  45.7 4.9 %tanh_add_fusion.5 = f32[1024,512]{1,0:T(8,128)S(1)} fusion(f32[1024,512]{1,0:T(8,128)S(1)} %tanh_add_fusion.6, f32[1024,512]{1,0:T(8,128)S(1)} %fusion.43, f32[1024,512]{1,0:T(8,128)S(1)} %collective-permute-done.1, f32[512]{0:T(512)S(1)} %bitcast.103, f32[2,3,2,512,512]{4,3,2,1,0:T(8,128)} %param.8), kind=kOutput, calls=%fused_computation.26 | convolution fusion | flops 3222798336 | bytes 9439232 | tf_op jit(solution)/shard_map/dot_general | solution.py:16
  50.6 24.9 %collective-permute-start.2 = (f32[1024,512]{1,0:T(8,128)S(1)}, f32[1024,512]{1,0:T(8,128)S(1)}, u32[]{:S(2)}, u32[]{:S(2)}) collective-permute-start(f32[1024,512]{1,0:T(8,128)S(1)} %tanh_add_fusion.5), channel_id=1, source_target_pairs={{0,2},{1,3},{2,4},{3,5},{4,6},{5,7},{6,8},{7,9},{8,10},{9,11},{10,... | collective-permute-start | bytes 6291464 | tf_op jit(solution)/shard_map/ppermute | solution.py:12
  75.6 4.7 %fusion.40 = f32[1024,512]{1,0:T(8,128)S(1)} fusion(f32[1024,512]{1,0:T(8,128)S(1)} %tanh_add_fusion.5, f32[2,3,2,512,512]{4,3,2,1,0:T(8,128)} %param.8), kind=kOutput, calls=%fused_computation.46 | convolution fusion | flops 3221225472 | bytes 5242880 | tf_op jit(solution)/shard_map/dot_general | solution.py:16
  80.3 39.1 %collective-permute-done.2 = f32[1024,512]{1,0:T(8,128)S(1)} collective-permute-done((f32[1024,512]{1,0:T(8,128)S(1)}, f32[1024,512]{1,0:T(8,128)S(1)}, u32[]{:S(2)}, u32[]{:S(2)}) %collective-permute-start.2) | collective-permute-done | bytes 2097184 | tf_op jit(solution)/shard_map/ppermute | solution.py:12
  119.4 5.1 %tanh_add_fusion.4 = f32[1024,512]{1,0:T(8,128)S(1)} fusion(f32[1024,512]{1,0:T(8,128)S(1)} %tanh_add_fusion.5, f32[1024,512]{1,0:T(8,128)S(1)} %fusion.40, f32[1024,512]{1,0:T(8,128)S(1)} %collective-permute-done.2, f32[512]{0:T(512)S(1)} %bitcast.100, f32[2,3,2,512,512]{4,3,2,1,0:T(8,128)} %param.8), kind=kOutput, calls=%fused_computation.25 | convolution fusion | flops 3222798336 | bytes 9439232 | tf_op jit(solution)/shard_map/dot_general | solution.py:16
  124.5 4.8 %add_tanh_fusion.1 = f32[1024,512]{1,0:T(8,128)} fusion(f32[1024,512]{1,0:T(8,128)S(1)} %tanh_add_fusion.4, f32[512]{0:T(512)S(1)} %bitcast.104, f32[2,512,512]{2,1,0:T(8,128)S(1)} %copy-done.5), kind=kOutput, calls=%fused_computation.24 | convolution fusion | flops 3221749760 | bytes 5244928 | tf_op jit(solution)/shard_map/dot_general | solution.py:16
  129.8 88.7 %all-reduce.3.cloned.1.call-done = f32[1024,512]{1,0:T(8,128)} async-done(((f32[1024,512]{1,0:T(8,128)}), f32[1024,512]{1,0:T(8,128)}) %all-reduce.3.cloned.1.call-update) | async-done | bytes 2097168 | tf_op jit(solution)/shard_map/psum | solution.py:57
  218.5 5.5 %fusion.16 = f32[1024,512]{1,0:T(8,128)S(1)} fusion(f32[1024,512]{1,0:T(8,128)} %all-reduce.3.cloned.1.call-done, f32[2,512,512]{2,1,0:T(8,128)} %param.11), kind=kOutput, calls=%fused_computation.22 | convolution fusion | flops 3221749760 | bytes 5242880 | tf_op jit(solution)/shard_map/dot_general | solution.py:16
  224.0 3.6 fusion.13
  227.6 3.7 tanh_add_fusion.3
  231.3 1.6 collective-permute-start.3
  233.0 4.7 %fusion.33 = f32[1024,512]{1,0:T(8,128)S(1)} fusion(f32[1024,512]{1,0:T(8,128)S(1)} %tanh_add_fusion.3, f32[2,3,2,512,512]{4,3,2,1,0:T(8,128)} %param.8), kind=kOutput, calls=%fused_computation.39 | convolution fusion | flops 3221225472 | bytes 5242880 | tf_op jit(solution)/shard_map/dot_general | solution.py:16
  237.8 5.0 %tanh_add_fusion.2 = f32[1024,512]{1,0:T(8,128)S(1)} fusion(f32[1024,512]{1,0:T(8,128)S(1)} %tanh_add_fusion.3, f32[1024,512]{1,0:T(8,128)S(1)} %fusion.33, f32[512,512]{1,0:T(8,128)S(1)} %slice.180, f32[512,512]{1,0:T(8,128)S(1)} %slice.179, f32[512]{0:T(512)S(1)} %bitcast.98, f32[2,3,2,512,512]{4,3,2,1,0:T(8,128)} %param.8), kind=kOutput, calls=%fused_computation.17 | convolution fusion | flops 3223322624 | bytes 9439232 | tf_op jit(solution)/shard_map/dot_general | solution.py:16
  242.8 22.1 %collective-permute-start.4 = (f32[1024,512]{1,0:T(8,128)S(1)}, f32[1024,512]{1,0:T(8,128)S(1)}, u32[]{:S(2)}, u32[]{:S(2)}) collective-permute-start(f32[1024,512]{1,0:T(8,128)S(1)} %tanh_add_fusion.2), channel_id=1, source_target_pairs={{0,1},{1,2},{2,3},{3,4},{4,5},{5,6},{6,7},{7,8},{8,9},{9,10},{10,1... | collective-permute-start | bytes 6291464 | tf_op jit(solution)/shard_map/ppermute | solution.py:12
  264.9 4.7 %fusion.30 = f32[1024,512]{1,0:T(8,128)S(1)} fusion(f32[1024,512]{1,0:T(8,128)S(1)} %tanh_add_fusion.2, f32[2,3,2,512,512]{4,3,2,1,0:T(8,128)} %param.8), kind=kOutput, calls=%fused_computation.36 | convolution fusion | flops 3221225472 | bytes 5242880 | tf_op jit(solution)/shard_map/dot_general | solution.py:16
  269.6 4.9 %tanh_add_fusion.1 = f32[1024,512]{1,0:T(8,128)S(1)} fusion(f32[1024,512]{1,0:T(8,128)S(1)} %tanh_add_fusion.2, f32[1024,512]{1,0:T(8,128)S(1)} %fusion.30, f32[1024,512]{1,0:T(8,128)S(1)} %collective-permute-done.4, f32[512]{0:T(512)S(1)} %bitcast.95, f32[2,3,2,512,512]{4,3,2,1,0:T(8,128)} %param.8), kind=kOutput, calls=%fused_computation.16 | convolution fusion | flops 3222798336 | bytes 9439232 | tf_op jit(solution)/shard_map/dot_general | solution.py:16
  274.6 25.2 %collective-permute-start.5 = (f32[1024,512]{1,0:T(8,128)S(1)}, f32[1024,512]{1,0:T(8,128)S(1)}, u32[]{:S(2)}, u32[]{:S(2)}) collective-permute-start(f32[1024,512]{1,0:T(8,128)S(1)} %tanh_add_fusion.1), channel_id=1, source_target_pairs={{0,2},{1,3},{2,4},{3,5},{4,6},{5,7},{6,8},{7,9},{8,10},{9,11},{10,... | collective-permute-start | bytes 6291464 | tf_op jit(solution)/shard_map/ppermute | solution.py:12
  299.8 4.7 %fusion.27 = f32[1024,512]{1,0:T(8,128)S(1)} fusion(f32[1024,512]{1,0:T(8,128)S(1)} %tanh_add_fusion.1, f32[2,3,2,512,512]{4,3,2,1,0:T(8,128)} %param.8), kind=kOutput, calls=%fused_computation.33 | convolution fusion | flops 3221225472 | bytes 5242880 | tf_op jit(solution)/shard_map/dot_general | solution.py:16
  304.5 39.1 %collective-permute-done.5 = f32[1024,512]{1,0:T(8,128)S(1)} collective-permute-done((f32[1024,512]{1,0:T(8,128)S(1)}, f32[1024,512]{1,0:T(8,128)S(1)}, u32[]{:S(2)}, u32[]{:S(2)}) %collective-permute-start.5) | collective-permute-done | bytes 2097184 | tf_op jit(solution)/shard_map/ppermute | solution.py:12
  343.6 5.1 %tanh_add_fusion = f32[1024,512]{1,0:T(8,128)S(1)} fusion(f32[1024,512]{1,0:T(8,128)S(1)} %tanh_add_fusion.1, f32[1024,512]{1,0:T(8,128)S(1)} %fusion.27, f32[1024,512]{1,0:T(8,128)S(1)} %collective-permute-done.5, f32[512]{0:T(512)S(1)} %bitcast.94, f32[2,3,2,512,512]{4,3,2,1,0:T(8,128)} %param.8), kind=kOutput, calls=%fused_computation.15 | convolution fusion | flops 3222798336 | bytes 9439232 | tf_op jit(solution)/shard_map/dot_general | solution.py:16
  348.7 4.8 %add_tanh_fusion = f32[1024,512]{1,0:T(8,128)} fusion(f32[1024,512]{1,0:T(8,128)S(1)} %tanh_add_fusion, f32[512]{0:T(512)S(1)} %bitcast.99, f32[2,512,512]{2,1,0:T(8,128)S(1)} %copy-done.6), kind=kOutput, calls=%fused_computation.14 | convolution fusion | flops 3221749760 | bytes 5244928 | tf_op jit(solution)/shard_map/dot_general | solution.py:16
  353.5 87.3 %all-reduce.5.cloned.1.call-done = f32[1024,512]{1,0:T(8,128)} async-done(((f32[1024,512]{1,0:T(8,128)}), f32[1024,512]{1,0:T(8,128)}) %all-reduce.5.cloned.1.call-update) | async-done | bytes 2097168 | tf_op jit(solution)/shard_map/psum | solution.py:57
  440.8 5.7 %fusion.11 = f32[1024,512]{1,0:T(8,128)S(1)} fusion(f32[1024,512]{1,0:T(8,128)} %all-reduce.5.cloned.1.call-done, f32[2,512,512]{2,1,0:T(8,128)} %param.11), kind=kOutput, calls=%fused_computation.12 | convolution fusion | flops 3221749760 | bytes 5242880 | tf_op jit(solution)/shard_map/dot_general | solution.py:16
  446.5 3.5 fusion.8
  450.1 5.0 %add_bitcast_fusion = f32[1,1024,512]{2,1,0:T(8,128)} fusion(f32[1024,512]{1,0:T(8,128)S(1)} %tanh_add_fusion, f32[1024,512]{1,0:T(8,128)S(1)} %fusion.8, f32[1024,512]{1,0:T(8,128)S(1)} %copy-done.1, f32[512]{0:T(512)S(1)} %bitcast.96, f32[2,1024,512]{2,1,0:T(8,128)S(1)} %copy-done.4), kind=kOutput, calls=%fused_computation.8 | convolution fusion | flops 3222798336 | bytes 9439232 | tf_op jit(solution)/shard_map/dot_general | solution.py:16
  (28 shorter events, 0.8 us)
Async XLA Ops:
  6.5 3.6 copy-start.2
  6.5 212.0 %all-reduce.3.cloned.1.call-start = ((), (), s32[]{:S(2)}) async-start(), calls=%async_computation | async-start | bytes 4194304 | tf_op jit(solution)/shard_map/psum | solution.py:57
  6.5 8.3 %collective-permute-start = (f32[1024,512]{1,0:T(8,128)}, f32[1024,512]{1,0:T(8,128)S(1)}, u32[]{:S(2)}, u32[]{:S(2)}) collective-permute-start(f32[1024,512]{1,0:T(8,128)} %bitcast.93), channel_id=1, source_target_pairs={{0,1},{1,2},{2,3},{3,4},{4,5},{5,6},{6,7},{7,8},{8,9},{9,10},{10,1... | collective-permute-start | bytes 6291464 | tf_op jit(solution)/shard_map/ppermute | solution.py:12
  19.9 25.7 %collective-permute-start.1 = (f32[1024,512]{1,0:T(8,128)S(1)}, f32[1024,512]{1,0:T(8,128)S(1)}, u32[]{:S(2)}, u32[]{:S(2)}) collective-permute-start(f32[1024,512]{1,0:T(8,128)S(1)} %tanh_add_fusion.6), channel_id=1, source_target_pairs={{0,1},{1,2},{2,3},{3,4},{4,5},{5,6},{6,7},{7,8},{8,9},{9,10},{10,1... | collective-permute-start | bytes 6291464 | tf_op jit(solution)/shard_map/ppermute | solution.py:12
  45.6 29.9 %copy-start.7 = (f32[2,3,512]{2,0,1:T(2,128)S(1)}, f32[2,3,512]{2,0,1:T(2,128)}, u32[]{:S(2)}) copy-start(f32[2,3,512]{2,0,1:T(2,128)} %param.13) | copy-start | bytes 36868
  50.6 68.8 %collective-permute-start.2 = (f32[1024,512]{1,0:T(8,128)S(1)}, f32[1024,512]{1,0:T(8,128)S(1)}, u32[]{:S(2)}, u32[]{:S(2)}) collective-permute-start(f32[1024,512]{1,0:T(8,128)S(1)} %tanh_add_fusion.5), channel_id=1, source_target_pairs={{0,2},{1,3},{2,4},{3,5},{4,6},{5,7},{6,8},{7,9},{8,10},{9,11},{10,... | collective-permute-start | bytes 6291464 | tf_op jit(solution)/shard_map/ppermute | solution.py:12
  119.4 5.1 %copy-start.5 = (f32[2,512,512]{2,1,0:T(8,128)S(1)}, f32[2,512,512]{2,1,0:T(8,128)}, u32[]{:S(2)}) copy-start(f32[2,512,512]{2,1,0:T(8,128)} %param.10) | copy-start | bytes 6291460
  129.3 311.5 %all-reduce.5.cloned.1.call-start = ((), (), s32[]{:S(2)}) async-start(), calls=%async_computation.1 | async-start | bytes 4194304 | tf_op jit(solution)/shard_map/psum | solution.py:57
  218.5 5.5 %copy-start.3 = (f32[2,1024,512]{2,1,0:T(8,128)S(1)}, f32[2,1024,512]{2,1,0:T(8,128)}, u32[]{:S(2)}) copy-start(f32[2,1024,512]{2,1,0:T(8,128)} %param.12) | copy-start | bytes 12582916
  224.0 3.6 copy-start
  231.3 6.4 %collective-permute-start.3 = (f32[1024,512]{1,0:T(8,128)S(1)}, f32[1024,512]{1,0:T(8,128)S(1)}, u32[]{:S(2)}, u32[]{:S(2)}) collective-permute-start(f32[1024,512]{1,0:T(8,128)S(1)} %tanh_add_fusion.3), channel_id=1, source_target_pairs={{0,1},{1,2},{2,3},{3,4},{4,5},{5,6},{6,7},{7,8},{8,9},{9,10},{10,1... | collective-permute-start | bytes 6291464 | tf_op jit(solution)/shard_map/ppermute | solution.py:12
  242.8 26.8 %collective-permute-start.4 = (f32[1024,512]{1,0:T(8,128)S(1)}, f32[1024,512]{1,0:T(8,128)S(1)}, u32[]{:S(2)}, u32[]{:S(2)}) collective-permute-start(f32[1024,512]{1,0:T(8,128)S(1)} %tanh_add_fusion.2), channel_id=1, source_target_pairs={{0,1},{1,2},{2,3},{3,4},{4,5},{5,6},{6,7},{7,8},{8,9},{9,10},{10,1... | collective-permute-start | bytes 6291464 | tf_op jit(solution)/shard_map/ppermute | solution.py:12
  274.6 69.0 %collective-permute-start.5 = (f32[1024,512]{1,0:T(8,128)S(1)}, f32[1024,512]{1,0:T(8,128)S(1)}, u32[]{:S(2)}, u32[]{:S(2)}) collective-permute-start(f32[1024,512]{1,0:T(8,128)S(1)} %tanh_add_fusion.1), channel_id=1, source_target_pairs={{0,2},{1,3},{2,4},{3,5},{4,6},{5,7},{6,8},{7,9},{8,10},{9,11},{10,... | collective-permute-start | bytes 6291464 | tf_op jit(solution)/shard_map/ppermute | solution.py:12
  343.6 5.1 %copy-start.6 = (f32[2,512,512]{2,1,0:T(8,128)S(1)}, f32[2,512,512]{2,1,0:T(8,128)}, u32[]{:S(2)}) copy-start(f32[2,512,512]{2,1,0:T(8,128)} %param.10) | copy-start | bytes 6291460
  440.8 5.8 %copy-start.4 = (f32[2,1024,512]{2,1,0:T(8,128)S(1)}, f32[2,1024,512]{2,1,0:T(8,128)}, u32[]{:S(2)}) copy-start(f32[2,1024,512]{2,1,0:T(8,128)} %param.12) | copy-start | bytes 12582916
  446.5 3.5 copy-start.1
Sparse Core Ops, SparseCore 0:
  129.4 89.0 all-reduce.2
  353.6 87.1 all-reduce.4
where the time goes:
time: 469 us; the launch traced here: 462 us
  waiting for transfers between devices  254 us (54%)
  starting transfers between devices  96.9 us (21%)
  matrix products  94.6 us (20%)
  between operations  14.2 us (3%)
    psum x2, waiting for transfers between devices, body(): summed = lax.psum(mapped, 'mic')  176 us
    ppermute x6, starting transfers between devices, from_behind(): return lax.ppermute(x, axis, pairs)  96.4 us
    dot_general x20, matrix products, matmul(): jnp.dot(left, right, precision=lax.Precision.HIGHEST, preferred_element_t...  94.6 us
    ppermute x6, waiting for transfers between devices, from_behind(): return lax.ppermute(x, axis, pairs)  78.2 us
  transfers between devices with their start and end apart: 8, of which 4 were waited for; matrix products, arithmetic and copies ran while one was open for 7% of the time, Pallas kernels for 0%

commit v1 on v0

--- a/solution.py
+++ b/solution.py
@@ -54,7 +54,7 @@
             matmul(hidden_activations, transform_in[section_index])
             + transform_offsets_bias[section_index, 0]
         )
-        summed = lax.psum(mapped, "mic")
+        summed = jnp.sum(lax.all_gather(mapped, "mic"), axis=0)
         pooled = jnp.tanh(
             matmul(summed / micro_count, transform_mid[section_index])
             + transform_offsets_bias[section_index, 1]

time: 469 us -> 663 us (1.41)
  waiting for transfers between devices: 254 us -> 429 us
  other arithmetic: 0 us -> 19.1 us
    all_gather x0 -> x2, waiting for transfers between devices: none -> 351 us  [body(): summed = jnp.sum(lax.all_gather(mapped, 'mic'), axis=0)]
    psum x2 -> x0, waiting for transfers between devices: 176 us -> none  [body(): summed = lax.psum(mapped, 'mic')]
    reduce_sum x0 -> x2, other arithmetic: none -> 19.1 us  [body(): summed = jnp.sum(lax.all_gather(mapped, 'mic'), axis=0)]
  transfers between devices with their start and end apart: 8 -> 8, of which waited for: 4 -> 4; matrix products, arithmetic and copies ran while one was open for 7% -> 5% of each run, Pallas kernels for 0% -> 0%
where the time goes in v1:
time: 663 us; the launch traced here: 656 us
  waiting for transfers between devices  429 us (65%)
  starting transfers between devices  96.8 us (15%)
  matrix products  94.4 us (14%)
  other arithmetic  19.1 us (3%)
  between operations  14.2 us (2%)
    all_gather x2, waiting for transfers between devices, body(): summed = jnp.sum(lax.all_gather(mapped, 'mic'), axis=0)  351 us
    ppermute x6, starting transfers between devices, from_behind(): return lax.ppermute(x, axis, pairs)  96.4 us
    dot_general x20, matrix products, matmul(): jnp.dot(left, right, precision=lax.Precision.HIGHEST, preferred_element_t...  94.4 us
    ppermute x6, waiting for transfers between devices, from_behind(): return lax.ppermute(x, axis, pairs)  78.3 us
    reduce_sum x2, other arithmetic, body(): summed = jnp.sum(lax.all_gather(mapped, 'mic'), axis=0)  19.1 us
  transfers between devices with their start and end apart: 8, of which 4 were waited for; matrix products, arithmetic and copies ran while one was open for 5% of the time, Pallas kernels for 0%

profile of v1, /device:TPU:0, one launch (start us, length us, event | category | flops | bytes accessed | tf_op | source)
XLA Modules:
  0.0 656.2 jit_solution(14769996941360824176)
XLA Ops:
  6.5 1.5 collective-permute-start
  10.2 4.7 fusion.46
  15.0 4.9 tanh_add_fusion.6
  19.9 21.0 %collective-permute-start.1 = (f32[1024,512]{1,0:T(8,128)S(1)}, f32[1024,512]{1,0:T(8,128)S(1)}, u32[]{:S(2)}, u32[]{:S(2)}) collective-permute-start(f32[1024,512]{1,0:T(8,128)S(1)} %tanh_add_fusion.6), channel_id=1, source_target_pairs={{0,1},{1,2},{2,3},{3,4},{4,5},{5,6},{6,7},{7,8},{8,9},{9,10},{10,1... | collective-permute-start | bytes 6291464 | tf_op jit(solution)/shard_map/ppermute | solution.py:12
  40.9 4.7 fusion.43
  45.6 5.0 tanh_add_fusion.5
  50.6 24.9 %collective-permute-start.2 = (f32[1024,512]{1,0:T(8,128)S(1)}, f32[1024,512]{1,0:T(8,128)S(1)}, u32[]{:S(2)}, u32[]{:S(2)}) collective-permute-start(f32[1024,512]{1,0:T(8,128)S(1)} %tanh_add_fusion.5), channel_id=1, source_target_pairs={{0,2},{1,3},{2,4},{3,5},{4,6},{5,7},{6,8},{7,9},{8,10},{9,11},{10,... | collective-permute-start | bytes 6291464 | tf_op jit(solution)/shard_map/ppermute | solution.py:12
  75.5 4.7 fusion.40
  80.2 39.2 %collective-permute-done.2 = f32[1024,512]{1,0:T(8,128)S(1)} collective-permute-done((f32[1024,512]{1,0:T(8,128)S(1)}, f32[1024,512]{1,0:T(8,128)S(1)}, u32[]{:S(2)}, u32[]{:S(2)}) %collective-permute-start.2) | collective-permute-done | bytes 2097184 | tf_op jit(solution)/shard_map/ppermute | solution.py:12
  119.4 5.1 tanh_add_fusion.4
  124.5 4.8 add_tanh_fusion.1
  129.8 177.0 %all-gather.5.cloned.1.call-done = f32[8192,512]{1,0:T(8,128)} async-done(((f32[1024,512]{1,0:T(8,128)}), f32[8192,512]{1,0:T(8,128)}) %all-gather.5.cloned.1.call-update) | async-done | bytes 16777232 | tf_op jit(solution)/shard_map/all_gather | solution.py:57
  306.8 9.4 %reduce_sum.18 = f32[1024,512]{1,0:T(8,128)} reduce(f32[8,1024,512]{2,1,0:T(8,128)} %bitcast.95, f32[]{:T(128)} %constant.4.clone.1), dimensions={0}, to_apply=%region_0.0 | reduce | flops 3670016 | bytes 18874372 | tf_op jit(solution)/shard_map/reduce_sum | solution.py:57
  316.2 5.5 fusion.16
  321.7 3.6 fusion.13
  325.2 3.7 tanh_add_fusion.3
  329.0 1.9 collective-permute-start.3
  330.9 4.7 fusion.33
  335.7 5.0 tanh_add_fusion.2
  340.7 21.8 %collective-permute-start.4 = (f32[1024,512]{1,0:T(8,128)S(1)}, f32[1024,512]{1,0:T(8,128)S(1)}, u32[]{:S(2)}, u32[]{:S(2)}) collective-permute-start(f32[1024,512]{1,0:T(8,128)S(1)} %tanh_add_fusion.2), channel_id=1, source_target_pairs={{0,1},{1,2},{2,3},{3,4},{4,5},{5,6},{6,7},{7,8},{8,9},{9,10},{10,1... | collective-permute-start | bytes 6291464 | tf_op jit(solution)/shard_map/ppermute | solution.py:12
  362.5 4.7 fusion.30
  367.2 4.9 tanh_add_fusion.1
  372.2 25.2 %collective-permute-start.5 = (f32[1024,512]{1,0:T(8,128)S(1)}, f32[1024,512]{1,0:T(8,128)S(1)}, u32[]{:S(2)}, u32[]{:S(2)}) collective-permute-start(f32[1024,512]{1,0:T(8,128)S(1)} %tanh_add_fusion.1), channel_id=1, source_target_pairs={{0,2},{1,3},{2,4},{3,5},{4,6},{5,7},{6,8},{7,9},{8,10},{9,11},{10,... | collective-permute-start | bytes 6291464 | tf_op jit(solution)/shard_map/ppermute | solution.py:12
  397.4 4.7 fusion.27
  402.1 39.1 %collective-permute-done.5 = f32[1024,512]{1,0:T(8,128)S(1)} collective-permute-done((f32[1024,512]{1,0:T(8,128)S(1)}, f32[1024,512]{1,0:T(8,128)S(1)}, u32[]{:S(2)}, u32[]{:S(2)}) %collective-permute-start.5) | collective-permute-done | bytes 2097184 | tf_op jit(solution)/shard_map/ppermute | solution.py:12
  441.2 5.1 tanh_add_fusion
  446.3 4.8 add_tanh_fusion
  451.1 174.1 %all-gather.7.cloned.1.call-done = f32[8192,512]{1,0:T(8,128)} async-done(((f32[1024,512]{1,0:T(8,128)}), f32[8192,512]{1,0:T(8,128)}) %all-gather.7.cloned.1.call-update) | async-done | bytes 16777232 | tf_op jit(solution)/shard_map/all_gather | solution.py:57
  625.2 9.7 %reduce_sum.19 = f32[1024,512]{1,0:T(8,128)} reduce(f32[8,1024,512]{2,1,0:T(8,128)} %bitcast.96, f32[]{:T(128)} %constant.4.clone.1), dimensions={0}, to_apply=%region_1.0 | reduce | flops 3670016 | bytes 18874372 | tf_op jit(solution)/shard_map/reduce_sum | solution.py:57
  634.8 5.5 fusion.11
  640.3 3.5 fusion.8
  643.9 5.0 add_bitcast_fusion
  (30 shorter events, 2.8 us)
Async XLA Ops:
  6.5 3.6 copy-start.2
  6.5 300.2 %all-gather.5.cloned.1.call-start = ((), (), s32[]{:S(2)}) async-start(), calls=%async_computation | async-start | bytes 18874368 | tf_op jit(solution)/shard_map/all_gather | solution.py:57
  6.5 8.3 %collective-permute-start = (f32[1024,512]{1,0:T(8,128)}, f32[1024,512]{1,0:T(8,128)S(1)}, u32[]{:S(2)}, u32[]{:S(2)}) collective-permute-start(f32[1024,512]{1,0:T(8,128)} %bitcast.97), channel_id=1, source_target_pairs={{0,1},{1,2},{2,3},{3,4},{4,5},{5,6},{6,7},{7,8},{8,9},{9,10},{10,1... | collective-permute-start | bytes 6291464 | tf_op jit(solution)/shard_map/ppermute | solution.py:12
  19.9 25.7 %collective-permute-start.1 = (f32[1024,512]{1,0:T(8,128)S(1)}, f32[1024,512]{1,0:T(8,128)S(1)}, u32[]{:S(2)}, u32[]{:S(2)}) collective-permute-start(f32[1024,512]{1,0:T(8,128)S(1)} %tanh_add_fusion.6), channel_id=1, source_target_pairs={{0,1},{1,2},{2,3},{3,4},{4,5},{5,6},{6,7},{7,8},{8,9},{9,10},{10,1... | collective-permute-start | bytes 6291464 | tf_op jit(solution)/shard_map/ppermute | solution.py:12
  45.6 29.9 %copy-start.7 = (f32[2,3,512]{2,0,1:T(2,128)S(1)}, f32[2,3,512]{2,0,1:T(2,128)}, u32[]{:S(2)}) copy-start(f32[2,3,512]{2,0,1:T(2,128)} %param.13) | copy-start | bytes 36868
  50.6 68.8 %collective-permute-start.2 = (f32[1024,512]{1,0:T(8,128)S(1)}, f32[1024,512]{1,0:T(8,128)S(1)}, u32[]{:S(2)}, u32[]{:S(2)}) collective-permute-start(f32[1024,512]{1,0:T(8,128)S(1)} %tanh_add_fusion.5), channel_id=1, source_target_pairs={{0,2},{1,3},{2,4},{3,5},{4,6},{5,7},{6,8},{7,9},{8,10},{9,11},{10,... | collective-permute-start | bytes 6291464 | tf_op jit(solution)/shard_map/ppermute | solution.py:12
  119.4 5.1 copy-start.5
  129.3 495.9 %all-gather.7.cloned.1.call-start = ((), (), s32[]{:S(2)}) async-start(), calls=%async_computation.1 | async-start | bytes 18874368 | tf_op jit(solution)/shard_map/all_gather | solution.py:57
  316.2 5.5 copy-start.3
  321.7 3.6 copy-start
  329.0 6.7 %collective-permute-start.3 = (f32[1024,512]{1,0:T(8,128)S(1)}, f32[1024,512]{1,0:T(8,128)S(1)}, u32[]{:S(2)}, u32[]{:S(2)}) collective-permute-start(f32[1024,512]{1,0:T(8,128)S(1)} %tanh_add_fusion.3), channel_id=1, source_target_pairs={{0,1},{1,2},{2,3},{3,4},{4,5},{5,6},{6,7},{7,8},{8,9},{9,10},{10,1... | collective-permute-start | bytes 6291464 | tf_op jit(solution)/shard_map/ppermute | solution.py:12
  340.7 26.5 %collective-permute-start.4 = (f32[1024,512]{1,0:T(8,128)S(1)}, f32[1024,512]{1,0:T(8,128)S(1)}, u32[]{:S(2)}, u32[]{:S(2)}) collective-permute-start(f32[1024,512]{1,0:T(8,128)S(1)} %tanh_add_fusion.2), channel_id=1, source_target_pairs={{0,1},{1,2},{2,3},{3,4},{4,5},{5,6},{6,7},{7,8},{8,9},{9,10},{10,1... | collective-permute-start | bytes 6291464 | tf_op jit(solution)/shard_map/ppermute | solution.py:12
  372.2 69.0 %collective-permute-start.5 = (f32[1024,512]{1,0:T(8,128)S(1)}, f32[1024,512]{1,0:T(8,128)S(1)}, u32[]{:S(2)}, u32[]{:S(2)}) collective-permute-start(f32[1024,512]{1,0:T(8,128)S(1)} %tanh_add_fusion.1), channel_id=1, source_target_pairs={{0,2},{1,3},{2,4},{3,5},{4,6},{5,7},{6,8},{7,9},{8,10},{9,11},{10,... | collective-permute-start | bytes 6291464 | tf_op jit(solution)/shard_map/ppermute | solution.py:12
  441.2 5.1 copy-start.6
  634.8 5.5 copy-start.4
  640.3 3.6 copy-start.1
Sparse Core Ops, SparseCore 0:
  129.4 177.2 all-gather.4
  451.2 173.9 all-gather.6
